TPU v7x, 32 devices: a whole 2x2x4 slice. The times are simulated.
32 devices in a mesh: ctx: 8 (over z, y), wsh: 4 (over x, core).
Axes of the slice: x: 2, y: 2, z: 4, core: 2. Of those that a mesh axis runs over, the one named last changes fastest.
Arguments:
- tokens: bfloat16 [4, 1024, 2048], P('wsh', 'ctx'), may hold values from -6 to 6
- out_grad: bfloat16 [4, 1024, 2048], P('wsh', 'ctx'), may hold values from -6 to 6
- attn_weight: bfloat16 [4, 2048, 2048], P(None, None, 'wsh'), may hold values from -0.125 to 0.125
- mlp_weight: bfloat16 [3, 2048, 8192], P(None, None, 'wsh'), may hold values from -0.125 to 0.125
- norm_gains: bfloat16 [4, 2048], P(None, 'wsh'), may hold values from 0.25 to 1.75
- adapt_model: bfloat16 [11, 64, 2048], P(None, None, 'wsh'), may hold values from -0.125 to 0.125
- adapt_hidden: bfloat16 [3, 64, 8192], P(None, None, 'wsh'), may hold values from -0.0625 to 0.0625
- lengths: int32 [4], replicated, may hold values from 512 to 1024, as said below
- adapter_pick: int32 [4], replicated, may hold values from 0 to 3
- block_order: int32 [4, 16], P('wsh'), may hold values from 0 to 15, as said below
Outputs:
- layer_out: bfloat16 [4, 1024, 2048], P('wsh', 'ctx')
- input_grad: float32 [4, 1024, 2048], P('wsh', 'ctx')
- adapt_model_grad: float32 [11, 64, 2048], P(None, None, 'wsh')
- adapt_hidden_grad: float32 [3, 64, 8192], P(None, None, 'wsh')
Inputs may be any that keep to these rules, and one draw needn't show every extreme that they name: `lengths`: some sequence has exactly 1024 valid tokens. Each row of block_order is a permutation of the 16 blocks; the two blocks stored on one index of ctx are p and 15 - p for some p, in either order.
All inputs are finite; a program needn't handle non-finite values.
Results may differ from a plain program's by a relative error of at most 0.017.
Values may be sent and summed in bfloat16 or wider, within the bound.
No kernel may reach another device: no remote copies, remote signals or barrier semaphores. Data moves between devices by JAX's collectives and lax.ppermute only.
A program may use at most 512 MiB of HBM per device.

v0:
```python
import jax
import jax.numpy as jnp
from jax import lax
from jax.sharding import PartitionSpec as P

HEADS = 16
HEAD_DIM = 128
FF = 8192
RANK = 16
ADAPTERS = 4
NORM_EPS = 1e-06
ADAPTER_SCALE = 4.0
ROPE_BASE = 500000.0


def rms_scale(values):
    return lax.rsqrt(jnp.mean(values * values, axis=-1, keepdims=True) + NORM_EPS)


def norm_back(values, scale_rows, upstream):
    return scale_rows * upstream - values * scale_rows**3 * jnp.mean(
        upstream * values, axis=-1, keepdims=True
    )


def rotary_tables(positions, head_dim):
    half_dim = head_dim // 2
    frequency = ROPE_BASE ** (-(jnp.arange(half_dim, dtype=jnp.float32) * 2.0) / head_dim)
    angles = positions.astype(jnp.float32)[:, None] * frequency[None, :]
    return (jnp.cos(angles)[:, None, :], jnp.sin(angles)[:, None, :])


def rotate(values, tables, heads_total):
    cosine, sine_part = tables
    row_count = values.shape[0]
    shaped = values.reshape(row_count, heads_total, -1)
    half_dim = shaped.shape[-1] // 2
    first_half = shaped[..., :half_dim]
    second_half = shaped[..., half_dim:]
    turned = jnp.concatenate(
        [
            first_half * cosine - second_half * sine_part,
            second_half * cosine + first_half * sine_part,
        ],
        axis=-1,
    )
    return turned.reshape(row_count, -1)


def rotate_back(gradient, tables, heads_total):
    cosine, sine_part = tables
    row_count = gradient.shape[0]
    shaped = gradient.reshape(row_count, heads_total, -1)
    half_dim = shaped.shape[-1] // 2
    first_half = shaped[..., :half_dim]
    second_half = shaped[..., half_dim:]
    turned = jnp.concatenate(
        [
            first_half * cosine + second_half * sine_part,
            second_half * cosine - first_half * sine_part,
        ],
        axis=-1,
    )
    return turned.reshape(row_count, -1)


def pick_rows(stacked, onehot, adapters):
    part_count, col_count = (stacked.shape[0], stacked.shape[2])
    split_view = stacked.reshape(part_count, adapters, -1, col_count)
    return jnp.einsum(
        "kard,a->krd", split_view, onehot.astype(stacked.dtype), preferred_element_type=jnp.float32
    ).astype(stacked.dtype)


def per_device(
    tokens,
    out_grad,
    attn_weight,
    mlp_weight,
    norm_gains,
    adapt_model,
    adapt_hidden,
    lengths,
    adapter_pick,
    block_order,
):
    input_rows = tokens[0]
    row_count, model_dim = input_rows.shape
    block_rows = row_count // 2
    ctx_size = lax.axis_size("ctx")
    slot_rows = row_count * ctx_size
    heads_all = HEADS
    head_dim = HEAD_DIM
    adapters = ADAPTERS
    score_scale = head_dim ** (-0.5)
    seq_index = lax.axis_index("wsh")
    ctx_index = lax.axis_index("ctx")
    seq_length = lax.dynamic_index_in_dim(lengths, seq_index, keepdims=False)
    chosen = lax.dynamic_index_in_dim(adapter_pick, seq_index, keepdims=False)
    onehot = (jnp.arange(adapters) == chosen).astype(jnp.float32)
    all_positions = (
        block_order[0][:, None] * block_rows + jnp.arange(block_rows)[None, :]
    ).reshape(-1)
    own_positions = lax.dynamic_slice_in_dim(all_positions, ctx_index * row_count, row_count)
    valid_rows = (own_positions < seq_length).astype(jnp.float32)[:, None]
    tables = rotary_tables(own_positions, head_dim)
    key_allowed = (all_positions[None, :] <= own_positions[:, None]) & (
        all_positions[None, :] < seq_length
    )

    def heads_view(matrix):
        return matrix.reshape(matrix.shape[0], heads_all, head_dim)

    attn_full, gains_full, adapt_full = (
        lax.all_gather(attn_weight, "wsh", axis=2, tiled=True),
        lax.all_gather(norm_gains, "wsh", axis=1, tiled=True),
        lax.all_gather(adapt_model, "wsh", axis=2, tiled=True),
    )
    gain_rows = gains_full.astype(jnp.float32)
    model_reduced = pick_rows(adapt_full, onehot, adapters)
    projected_rows = jnp.einsum(
        "td,kde->kte", input_rows, attn_full[:3], preferred_element_type=jnp.float32
    )
    low_in = jnp.einsum(
        "td,krd->ktr", input_rows, model_reduced[:3], preferred_element_type=jnp.float32
    ).astype(jnp.bfloat16)
    projected_rows = projected_rows + ADAPTER_SCALE * jnp.einsum(
        "ktr,krd->ktd", low_in, model_reduced[6:9], preferred_element_type=jnp.float32
    )
    query_scale = rms_scale(projected_rows[0])
    key_scale = rms_scale(projected_rows[1])
    queries = rotate(projected_rows[0] * query_scale * gain_rows[0], tables, heads_all).astype(
        jnp.bfloat16
    )
    own_keys = rotate(projected_rows[1] * key_scale * gain_rows[1], tables, heads_all).astype(
        jnp.bfloat16
    )
    own_values = projected_rows[2].astype(jnp.bfloat16)
    all_keys, all_values = (
        lax.all_gather(own_keys, "ctx", axis=0, tiled=True),
        lax.all_gather(own_values, "ctx", axis=0, tiled=True),
    )
    query_heads = heads_view(queries)
    key_heads = heads_view(all_keys)
    value_heads = heads_view(all_values)
    scores = (
        jnp.einsum("thd,shd->hts", query_heads, key_heads, preferred_element_type=jnp.float32)
        * score_scale
    )
    scores = jnp.where(key_allowed[None], scores, -jnp.inf)
    row_max = jnp.max(scores, axis=-1, keepdims=True)
    log_full = row_max + jnp.log(jnp.sum(jnp.exp(scores - row_max), axis=-1, keepdims=True))
    weights = jnp.exp(scores - log_full).astype(jnp.bfloat16)
    attended = (
        jnp.einsum("hts,shd->thd", weights, value_heads, preferred_element_type=jnp.float32)
        .reshape(row_count, model_dim)
        .astype(jnp.bfloat16)
    )
    log_totals = log_full[..., 0]
    reduced_output = jnp.einsum(
        "td,rd->tr", attended, model_reduced[3], preferred_element_type=jnp.float32
    ).astype(jnp.bfloat16)
    branch = jnp.dot(
        attended, attn_full[3], preferred_element_type=jnp.float32
    ) + ADAPTER_SCALE * jnp.dot(
        reduced_output, model_reduced[9], preferred_element_type=jnp.float32
    )
    branch_scale = rms_scale(branch)
    hidden_in = input_rows.astype(jnp.float32) + branch * branch_scale * gain_rows[2]
    hidden_low = hidden_in.astype(jnp.bfloat16)
    reduced_gate_up = jnp.einsum(
        "td,krd->ktr", hidden_low, model_reduced[4:6], preferred_element_type=jnp.float32
    ).astype(jnp.bfloat16)

    def gate_up_parts(weight_piece, gathered_rows):
        gate_part = jnp.dot(
            hidden_low, weight_piece[0], preferred_element_type=jnp.float32
        ) + ADAPTER_SCALE * jnp.dot(
            reduced_gate_up[0], gathered_rows[0], preferred_element_type=jnp.float32
        )
        up_part = jnp.dot(
            hidden_low, weight_piece[1], preferred_element_type=jnp.float32
        ) + ADAPTER_SCALE * jnp.dot(
            reduced_gate_up[1], gathered_rows[1], preferred_element_type=jnp.float32
        )
        return (gate_part, up_part)

    weight_piece = lax.all_gather(mlp_weight, "wsh", axis=2, tiled=True)
    adapt_piece = lax.all_gather(adapt_hidden, "wsh", axis=2, tiled=True)
    gathered_rows = pick_rows(adapt_piece, onehot, adapters)
    gate_part, up_part = gate_up_parts(weight_piece, gathered_rows)
    product = (jax.nn.silu(gate_part) * up_part).astype(jnp.bfloat16)
    down_total_sum = jnp.einsum(
        "tn,dn->td", product, weight_piece[2], preferred_element_type=jnp.float32
    )
    low_down_sum = jnp.einsum(
        "tn,rn->tr", product, gathered_rows[2], preferred_element_type=jnp.float32
    )
    down_total_sum, low_down_sum = (down_total_sum, low_down_sum)
    low_down = low_down_sum.astype(jnp.bfloat16)
    feedforward_output = down_total_sum + ADAPTER_SCALE * jnp.dot(
        low_down, model_reduced[10], preferred_element_type=jnp.float32
    )
    mlp_scale = rms_scale(feedforward_output)
    result = hidden_in + feedforward_output * mlp_scale * gain_rows[3]
    upstream = out_grad[0].astype(jnp.float32) * valid_rows
    grad_mlp_out = norm_back(feedforward_output, mlp_scale, upstream * gain_rows[3]).astype(
        jnp.bfloat16
    )
    grad_low_down = (
        ADAPTER_SCALE
        * jnp.einsum(
            "td,rd->tr", grad_mlp_out, model_reduced[10], preferred_element_type=jnp.float32
        )
    ).astype(jnp.bfloat16)
    gradient_down_factor = ADAPTER_SCALE * jnp.einsum(
        "tr,td->rd", low_down, grad_mlp_out, preferred_element_type=jnp.float32
    )
    weight_piece = lax.all_gather(mlp_weight, "wsh", axis=2, tiled=True)
    adapt_piece = lax.all_gather(adapt_hidden, "wsh", axis=2, tiled=True)
    gathered_rows = pick_rows(adapt_piece, onehot, adapters)
    gate_part, up_part = gate_up_parts(weight_piece, gathered_rows)
    sigmoid_gate = jax.nn.sigmoid(gate_part)
    silu_gate = gate_part * sigmoid_gate
    product = (silu_gate * up_part).astype(jnp.bfloat16)
    grad_product = jnp.dot(
        grad_mlp_out, weight_piece[2], preferred_element_type=jnp.float32
    ) + jnp.dot(grad_low_down, gathered_rows[2], preferred_element_type=jnp.float32)
    grad_gate = (
        grad_product * up_part * sigmoid_gate * (1.0 + gate_part * (1.0 - sigmoid_gate))
    ).astype(jnp.bfloat16)
    grad_up = (grad_product * silu_gate).astype(jnp.bfloat16)
    input_sum = jnp.einsum(
        "tn,dn->td", grad_gate, weight_piece[0], preferred_element_type=jnp.float32
    ) + jnp.einsum("tn,dn->td", grad_up, weight_piece[1], preferred_element_type=jnp.float32)
    reduced_sum = ADAPTER_SCALE * jnp.stack(
        [
            jnp.einsum(
                "tn,rn->tr", grad_gate, gathered_rows[0], preferred_element_type=jnp.float32
            ),
            jnp.einsum("tn,rn->tr", grad_up, gathered_rows[1], preferred_element_type=jnp.float32),
        ]
    )
    piece_grads = jnp.stack(
        [
            ADAPTER_SCALE
            * jnp.einsum(
                "tr,tn->rn", reduced_gate_up[0], grad_gate, preferred_element_type=jnp.float32
            ),
            ADAPTER_SCALE
            * jnp.einsum(
                "tr,tn->rn", reduced_gate_up[1], grad_up, preferred_element_type=jnp.float32
            ),
            jnp.einsum("tr,tn->rn", grad_low_down, product, preferred_element_type=jnp.float32),
        ]
    )
    input_sum, reduced_sum, picked_hidden = (input_sum, reduced_sum, piece_grads)
    low_grads = reduced_sum.astype(jnp.bfloat16)
    grad_hidden = (
        upstream
        + input_sum
        + jnp.einsum(
            "ktr,krd->td", low_grads, model_reduced[4:6], preferred_element_type=jnp.float32
        )
    )
    grad_a_gate_up = jnp.einsum(
        "ktr,td->krd", low_grads, hidden_low, preferred_element_type=jnp.float32
    )
    grad_branch = norm_back(branch, branch_scale, grad_hidden * gain_rows[2]).astype(jnp.bfloat16)
    grad_low_out = (
        ADAPTER_SCALE
        * jnp.einsum("td,rd->tr", grad_branch, model_reduced[9], preferred_element_type=jnp.float32)
    ).astype(jnp.bfloat16)
    gradient_output_factor = ADAPTER_SCALE * jnp.einsum(
        "tr,td->rd", reduced_output, grad_branch, preferred_element_type=jnp.float32
    )
    grad_a_out = jnp.einsum("tr,td->rd", grad_low_out, attended, preferred_element_type=jnp.float32)
    grad_attended = (
        jnp.einsum("te,de->td", grad_branch, attn_full[3], preferred_element_type=jnp.float32)
        + jnp.einsum(
            "tr,rd->td", grad_low_out, model_reduced[3], preferred_element_type=jnp.float32
        )
    ).astype(jnp.bfloat16)
    grad_heads = heads_view(grad_attended)
    scores = (
        jnp.einsum("thd,shd->hts", query_heads, key_heads, preferred_element_type=jnp.float32)
        * score_scale
    )
    scores = jnp.where(key_allowed[None], scores, -jnp.inf)
    weights_full = jnp.exp(scores - log_totals[..., None])
    grad_probs = jnp.einsum(
        "thd,shd->hts", grad_heads, value_heads, preferred_element_type=jnp.float32
    )
    row_delta = jnp.sum(weights_full * grad_probs, axis=-1, keepdims=True)
    grad_scores = (weights_full * (grad_probs - row_delta)).astype(jnp.bfloat16)
    grad_queries = (
        jnp.einsum("hts,shd->thd", grad_scores, key_heads, preferred_element_type=jnp.float32)
        * score_scale
    ).reshape(row_count, model_dim)
    key_full = (
        jnp.einsum("hts,thd->shd", grad_scores, query_heads, preferred_element_type=jnp.float32)
        * score_scale
    ).reshape(slot_rows, model_dim)
    value_full = jnp.einsum(
        "hts,thd->shd",
        weights_full.astype(jnp.bfloat16),
        grad_heads,
        preferred_element_type=jnp.float32,
    ).reshape(slot_rows, model_dim)
    grad_keys, grad_values = (
        lax.psum_scatter(key_full, "ctx", scatter_dimension=0, tiled=True),
        lax.psum_scatter(value_full, "ctx", scatter_dimension=0, tiled=True),
    )
    grad_proj_query = norm_back(
        projected_rows[0], query_scale, rotate_back(grad_queries, tables, heads_all) * gain_rows[0]
    ).astype(jnp.bfloat16)
    grad_proj_key = norm_back(
        projected_rows[1], key_scale, rotate_back(grad_keys, tables, heads_all) * gain_rows[1]
    ).astype(jnp.bfloat16)
    grad_proj = jnp.stack([grad_proj_query, grad_proj_key, grad_values.astype(jnp.bfloat16)])
    grad_low_qkv = (
        ADAPTER_SCALE
        * jnp.einsum(
            "ktd,krd->ktr", grad_proj, model_reduced[6:9], preferred_element_type=jnp.float32
        )
    ).astype(jnp.bfloat16)
    gradient_projection_factor = ADAPTER_SCALE * jnp.einsum(
        "ktr,ktd->krd", low_in, grad_proj, preferred_element_type=jnp.float32
    )
    grad_a_qkv = jnp.einsum(
        "ktr,td->krd", grad_low_qkv, input_rows, preferred_element_type=jnp.float32
    )
    grad_inputs = (
        grad_hidden
        + jnp.einsum("kte,kde->td", grad_proj, attn_full[:3], preferred_element_type=jnp.float32)
        + jnp.einsum(
            "ktr,krd->td", grad_low_qkv, model_reduced[:3], preferred_element_type=jnp.float32
        )
    )
    picked_model = jnp.concatenate(
        [
            grad_a_qkv,
            grad_a_out[None],
            grad_a_gate_up,
            gradient_projection_factor,
            gradient_output_factor[None],
            gradient_down_factor[None],
        ],
        axis=0,
    )
    spread_model = (onehot[None, :, None, None] * picked_model[:, None]).reshape(
        picked_model.shape[0], adapters * RANK, model_dim
    )
    spread_hidden = (onehot[None, :, None, None] * picked_hidden[:, None]).reshape(
        picked_hidden.shape[0], adapters * RANK, FF
    )
    shard_model, shard_hidden = (
        lax.psum_scatter(spread_model, "wsh", scatter_dimension=2, tiled=True),
        lax.psum_scatter(spread_hidden, "wsh", scatter_dimension=2, tiled=True),
    )
    model_grads, hidden_grads_out = lax.psum((shard_model, shard_hidden), "ctx")
    return (result.astype(jnp.bfloat16)[None], grad_inputs[None], model_grads, hidden_grads_out)


def solution(mesh):
    in_specs = (
        P("wsh", "ctx", None),
        P("wsh", "ctx", None),
        P(None, None, "wsh"),
        P(None, None, "wsh"),
        P(None, "wsh"),
        P(None, None, "wsh"),
        P(None, None, "wsh"),
        P(),
        P(),
        P("wsh", None),
    )
    out_specs = (
        P("wsh", "ctx", None),
        P("wsh", "ctx", None),
        P(None, None, "wsh"),
        P(None, None, "wsh"),
    )
    return jax.shard_map(
        per_device, mesh=mesh, in_specs=in_specs, out_specs=out_specs, check_vma=False
    )
```

profile of v0, /device:TPU:0, one launch (start us, length us, event | category | flops | bytes accessed | tf_op | source)
XLA Modules:
  0.0 1708.9 jit_solution(13489928325962978200)
XLA Ops:
  7.9 11.5 copy.32
  20.4 6.4 all_gather.26
  29.2 10.2 all-gather.10.cloned.1.call-done
  39.4 4.8 fusion.19
  45.8 196.8 %all-gather.8.cloned.1.call-done = bf16[4,2048,2048]{1,2,0:T(8,128)(2,1)} async-done(((bf16[4,2048,512]{1,2,0:T(8,128)(2,1)}), bf16[4,2048,2048]{1,2,0:T(8,128)(2,1)}) %all-gather.8.cloned.1.call-update) | async-done | bytes 33554448 | tf_op jit(solution)/shard_map/all_gather | solution.py:115
  242.6 11.9 fusion.74
  257.7 2.8 copy.34
  260.4 2.5 copy.35
  268.2 2.1 copy.36
  272.9 6.7 fusion.17
  281.4 67.9 %all-gather.12.cloned.1.call-done = bf16[1024,2048]{0,1:T(8,128)(2,1)} async-done(((bf16[128,2048]{0,1:T(8,128)(2,1)}), bf16[1024,2048]{0,1:T(8,128)(2,1)}) %all-gather.12.cloned.1.call-update) | async-done | bytes 4194320 | tf_op jit(solution)/shard_map/all_gather | solution.py:140
  349.3 4.3 fusion.14
  353.6 2.5 exponential_reduce_fusion
  356.9 67.7 %all-gather.18.cloned.1.call-done = bf16[1,1024,2048]{1,2,0:T(8,128)(2,1)} async-done(((bf16[1,128,2048]{1,2,0:T(8,128)(2,1)}), bf16[1,1024,2048]{1,2,0:T(8,128)(2,1)}) %all-gather.18.cloned.1.call-update) | async-done | bytes 4194320 | tf_op jit(solution)/shard_map/all_gather | solution.py:141
  424.6 7.2 convolution_convert_fusion
  432.0 9.3 fusion.13
  442.3 565.8 %all-gather.14.cloned.1.call-done = bf16[3,2048,8192]{2,1,0:T(8,128)(2,1)} async-done(((bf16[3,2048,2048]{2,1,0:T(8,128)(2,1)}), bf16[3,2048,8192]{2,1,0:T(8,128)(2,1)}) %all-gather.14.cloned.1.call-update) | async-done | bytes 100663312 | tf_op jit(solution)/shard_map/all_gather | solution.py:188
  1008.1 15.0 fusion.1
  1023.1 5.0 fusion.8
  1028.1 15.2 fusion.3
  1043.3 7.1 multiply_convert_fusion.3
  1052.2 15.8 fusion.5
  1070.0 15.2 fusion.4
  1085.2 7.1 multiply_convert_fusion.1
  1093.6 16.7 fusion
  1110.4 17.0 fusion.37
  1130.7 4.6 fusion.12
  1136.0 8.2 multiply_reduce_fusion
  1144.2 2.6 multiply_convert_fusion
  1146.8 4.7 broadcast_multiply_fusion
  1151.6 9.4 fusion.81
  1163.0 2.2 fusion.10
  1165.7 3.4 bitcast_multiply_fusion
  1169.1 4.8 fusion.45
  1173.9 125.7 %reduce-scatter.5.cloned.1.call-done = f32[128,2048]{0,1:T(8,128)} async-done(((f32[1024,2048]{0,1:T(8,128)}), f32[128,2048]{0,1:T(8,128)}) %reduce-scatter.5.cloned.1.call-update) | async-done | bytes 1048592 | tf_op jit(solution)/shard_map/reduce_scatter | solution.py:311
  1299.6 2.1 fusion.98
  1306.7 2.7 copy.41
  1309.4 3.0 pad_maximum_fusion.3
  1312.4 2.5 copy.46
  1316.9 133.3 %reduce-scatter.7.cloned.1.call-done = f32[128,2048]{0,1:T(8,128)} async-done(((f32[1024,2048]{0,1:T(8,128)}), f32[128,2048]{0,1:T(8,128)}) %reduce-scatter.7.cloned.1.call-update) | async-done | bytes 1048592 | tf_op jit(solution)/shard_map/reduce_scatter | solution.py:312
  1451.5 2.1 fusion.65
  1457.0 3.3 bitcast_multiply_fusion.1
  1460.4 49.5 %reduce-scatter.11.cloned.1.call-done = f32[3,64,2048]{2,1,0:T(8,128)} async-done(((f32[3,64,8192]{2,1,0:T(8,128)}), f32[3,64,2048]{2,1,0:T(8,128)}) %reduce-scatter.11.cloned.1.call-update) | async-done | bytes 1572880 | tf_op jit(solution)/shard_map/reduce_scatter | solution.py:359
  1509.8 57.0 %reduce-scatter.9.cloned.1.call-done = f32[11,64,512]{2,1,0:T(8,128)} async-done(((f32[11,64,2048]{2,1,0:T(8,128)}), f32[11,64,512]{2,1,0:T(8,128)}) %reduce-scatter.9.cloned.1.call-update) | async-done | bytes 1441808 | tf_op jit(solution)/shard_map/reduce_scatter | solution.py:358
  1568.1 11.3 fusion.32
  1579.4 117.3 %all-reduce.3.cloned.1.call-done = (f32[11,64,512]{2,1,0:T(8,128)}, f32[3,64,2048]{2,1,0:T(8,128)}) async-done(((f32[11,64,512]{2,1,0:T(8,128)}, f32[3,64,2048]{2,1,0:T(8,128)}), (f32[11,64,512]{2,1,0:T(8,128)}, f32[3,64,2048]{2,1,0:T(8,128)})) %all-reduce.3.cloned.1.call-update) | async-done | bytes 3014672 | tf_op jit(solution)/shard_map/psum | solution.py:361
  1696.7 2.6 copy.86
  1699.3 2.7 copy.87
  (214 shorter events, 44.5 us)
Async XLA Ops:
  7.2 32.2 %all-gather.10.cloned.1.call-start = ((), (), s32[]{:S(2)}) async-start(), calls=%async_computation.5 | async-start | bytes 3604480 | tf_op jit(solution)/shard_map/all_gather | solution.py:117
  7.9 234.7 %all-gather.8.cloned.1.call-start = ((), (), s32[]{:S(2)}) async-start(), calls=%async_computation.4 | async-start | bytes 41943040 | tf_op jit(solution)/shard_map/all_gather | solution.py:115
  19.5 7.4 copy-start.58
  19.5 8.8 copy-start.59
  19.5 253.4 %all-gather.16.cloned.1.call-start = ((), (), s32[]{:S(2)}) async-start(), calls=%async_computation.8 | async-start | bytes 3932160 | tf_op jit(solution)/shard_map/all_gather | solution.py:189
  20.2 329.1 %all-gather.12.cloned.1.call-start = ((), (), s32[]{:S(2)}) async-start(), calls=%async_computation.6 | async-start | bytes 4718592 | tf_op jit(solution)/shard_map/all_gather | solution.py:140
  26.9 236.9 %copy-start.42 = (f32[1,2048]{1,0:T(1,128)}, f32[1,2048]{1,0:T(1,128)S(1)}, u32[]{:S(2)}) copy-start(f32[1,2048]{1,0:T(1,128)S(1)} %get-tuple-element.38) | copy-start | bytes 24580
  26.9 238.3 %copy-start.44 = (f32[1,2048]{1,0:T(1,128)}, f32[1,2048]{1,0:T(1,128)S(1)}, u32[]{:S(2)}) copy-start(f32[1,2048]{1,0:T(1,128)S(1)} %get-tuple-element.39) | copy-start | bytes 24580
  29.1 236.3 %copy-start.32 = (f32[128,64]{1,0:T(8,128)}, f32[128,64]{1,0:T(8,128)S(1)}, u32[]{:S(2)}) copy-start(f32[128,64]{1,0:T(8,128)S(1)} %get-tuple-element.40) | copy-start | bytes 98308
  29.1 236.3 %copy-start.34 = (f32[128,64]{1,0:T(8,128)}, f32[128,64]{1,0:T(8,128)S(1)}, u32[]{:S(2)}) copy-start(f32[128,64]{1,0:T(8,128)S(1)} %get-tuple-element.41) | copy-start | bytes 98308
  39.4 6.1 copy-start.4
  45.8 208.7 %copy-start.46 = (bf16[3,16,128]{2,1,0:T(8,128)(2,1)}, bf16[3,16,128]{2,1,0:T(8,128)(2,1)S(1)}, u32[]{:S(2)}) copy-start(bf16[3,16,128]{2,1,0:T(8,128)(2,1)S(1)} %convolution_convert_fusion.1) | copy-start | bytes 36868
  256.1 14.3 copy-start.1
  270.3 154.3 %all-gather.18.cloned.1.call-start = ((), (), s32[]{:S(2)}) async-start(), calls=%async_computation.13 | async-start | bytes 4718592 | tf_op jit(solution)/shard_map/all_gather | solution.py:141
  271.3 736.9 %all-gather.14.cloned.1.call-start = ((), (), s32[]{:S(2)}) async-start(), calls=%async_computation.7 | async-start | bytes 125829120 | tf_op jit(solution)/shard_map/all_gather | solution.py:188
  271.8 1027.7 %reduce-scatter.5.cloned.1.call-start = ((), (), s32[]{:S(2)}) async-start(), calls=%async_computation.9 | async-start | bytes 9437184 | tf_op jit(solution)/shard_map/reduce_scatter | solution.py:311
  272.9 76.4 %copy-start.20 = (bf16[128,16,64]{2,0,1:T(8,128)(2,1)S(1)}, bf16[128,16,64]{2,0,1:T(8,128)(2,1)}, u32[]{:S(2)}) copy-start(bf16[128,16,64]{2,0,1:T(8,128)(2,1)} %get-tuple-element.24) | copy-start | bytes 786436
  272.9 76.4 %copy-start.22 = (bf16[128,16,64]{2,0,1:T(8,128)(2,1)S(1)}, bf16[128,16,64]{2,0,1:T(8,128)(2,1)}, u32[]{:S(2)}) copy-start(bf16[128,16,64]{2,0,1:T(8,128)(2,1)} %get-tuple-element.25) | copy-start | bytes 786436
  424.6 7.2 copy-start.13
  431.8 9.6 copy-start.28
  432.0 9.4 copy-start.48
  432.0 9.8 copy-start.5
  442.1 586.1 %copy-start.14 = (bf16[128,2048]{1,0:T(8,128)(2,1)}, bf16[128,2048]{1,0:T(8,128)(2,1)S(1)}, u32[]{:S(2)}) copy-start(bf16[128,2048]{1,0:T(8,128)(2,1)S(1)} %fusion.68) | copy-start | bytes 1572868
  1050.5 17.5 %copy-start.7 = (bf16[128,8192]{1,0:T(8,128)(2,1)}, bf16[128,8192]{1,0:T(8,128)(2,1)S(1)}, u32[]{:S(2)}) copy-start(bf16[128,8192]{1,0:T(8,128)(2,1)S(1)} %get-tuple-element.54) | copy-start | bytes 6291460
  1052.2 15.8 copy-start.30
  1085.2 7.1 copy-start.24
  1092.3 18.1 %copy-start.11 = (bf16[128,8192]{1,0:T(8,128)(2,1)}, bf16[128,8192]{1,0:T(8,128)(2,1)S(1)}, u32[]{:S(2)}) copy-start(bf16[128,8192]{1,0:T(8,128)(2,1)S(1)} %get-tuple-element.14) | copy-start | bytes 6291460
  1093.6 16.8 copy-start.31
  1130.4 4.9 copy-start.18
  1136.0 8.2 slice-start
  1136.0 8.2 slice-start.1
  1151.6 298.6 %reduce-scatter.7.cloned.1.call-start = ((), (), s32[]{:S(2)}) async-start(), calls=%async_computation.10 | async-start | bytes 9437184 | tf_op jit(solution)/shard_map/reduce_scatter | solution.py:312
  1161.0 348.8 %reduce-scatter.11.cloned.1.call-start = ((), (), s32[]{:S(2)}) async-start(), calls=%async_computation.12 | async-start | bytes 7864320 | tf_op jit(solution)/shard_map/reduce_scatter | solution.py:359
  1169.1 397.7 %reduce-scatter.9.cloned.1.call-start = ((), (), s32[]{:S(2)}) async-start(), calls=%async_computation.11 | async-start | bytes 7208960 | tf_op jit(solution)/shard_map/reduce_scatter | solution.py:358
  1173.9 129.5 %copy-start.33 = (f32[128,64]{1,0:T(8,128)S(1)}, f32[128,64]{1,0:T(8,128)}, u32[]{:S(2)}) copy-start(f32[128,64]{1,0:T(8,128)} %copy-done.32) | copy-start | bytes 98308
  1173.9 129.5 %copy-start.35 = (f32[128,64]{1,0:T(8,128)S(1)}, f32[128,64]{1,0:T(8,128)}, u32[]{:S(2)}) copy-start(f32[128,64]{1,0:T(8,128)} %copy-done.34) | copy-start | bytes 98308
  1306.7 8.2 copy-start.2
  1306.7 8.2 copy-start.43
  1306.7 8.2 copy-start.45
  1312.4 139.1 %copy-start.51 = (f32[128]{0:T(128)S(1)}, f32[128]{0:T(128)}, u32[]{:S(2)}) copy-start(f32[128]{0:T(128)} %copy-done.50) | copy-start | bytes 1540
  1312.4 139.1 %copy-start.53 = (f32[128]{0:T(128)S(1)}, f32[128]{0:T(128)}, u32[]{:S(2)}) copy-start(f32[128]{0:T(128)} %copy-done.52) | copy-start | bytes 1540
  1312.4 139.1 %copy-start.55 = (f32[128]{0:T(128)S(1)}, f32[128]{0:T(128)}, u32[]{:S(2)}) copy-start(f32[128]{0:T(128)} %get-tuple-element.44) | copy-start | bytes 1540
  1312.4 139.1 %copy-start.56 = (f32[128]{0:T(128)S(1)}, f32[128]{0:T(128)}, u32[]{:S(2)}) copy-start(f32[128]{0:T(128)} %get-tuple-element.62) | copy-start | bytes 1540
  1460.3 107.8 %copy-start.27 = (f32[128,2048]{1,0:T(8,128)S(1)}, f32[128,2048]{1,0:T(8,128)}, u32[]{:S(2)}) copy-start(f32[128,2048]{1,0:T(8,128)} %copy-done.26) | copy-start | bytes 3145732
  1460.3 107.8 %copy-start.37 = (bf16[1,128,2048]{1,2,0:T(8,128)(2,1)S(1)}, bf16[1,128,2048]{1,2,0:T(8,128)(2,1)}, u32[]{:S(2)}) copy-start(bf16[1,128,2048]{1,2,0:T(8,128)(2,1)} %copy-done.36) | copy-start | bytes 1572868
  1460.3 107.8 %copy-start.39 = (bf16[1,128,2048]{1,2,0:T(8,128)(2,1)S(1)}, bf16[1,128,2048]{1,2,0:T(8,128)(2,1)}, u32[]{:S(2)}) copy-start(bf16[1,128,2048]{1,2,0:T(8,128)(2,1)} %copy-done.38) | copy-start | bytes 1572868
  1460.3 107.8 %copy-start.41 = (bf16[1,128,2048]{1,2,0:T(8,128)(2,1)S(1)}, bf16[1,128,2048]{1,2,0:T(8,128)(2,1)}, u32[]{:S(2)}) copy-start(bf16[1,128,2048]{1,2,0:T(8,128)(2,1)} %copy-done.40) | copy-start | bytes 1572868
  1460.3 236.4 %all-reduce.3.cloned.1.call-start = ((), (), s32[]{:S(2)}) async-start(), calls=%async_computation.14 | async-start | bytes 6029312 | tf_op jit(solution)/shard_map/psum | solution.py:361
  (25 other events, 65.0 us)
Sparse Core Ops, SparseCore 0:
  9.5 29.8 all-gather.9
  41.0 201.5 all-gather.7
  244.1 28.4 all-gather.15
  274.6 74.6 all-gather.11
  351.8 72.8 all-gather.17
  426.0 582.0 all-gather.13
  1151.7 147.8 reduce-scatter.4
  1303.2 146.9 reduce-scatter.6
  1452.7 57.0 reduce-scatter.10
  1512.2 54.5 reduce-scatter.8
  1570.6 126.0 all-reduce.2
where the time goes:
time: 1720 us; the launch traced here: 1710 us
  waiting for transfers between devices  1390 us (81%)
  matrix products  217 us (13%)
  local copies, waits for them, and re-layouts  42.7 us (2%)
  other arithmetic  33.2 us (2%)
    all_gather x1, waiting for transfers between devices, per_device(): weight_piece = lax.all_gather(mlp_weight, 'wsh', axis=2, tiled=True)  566 us
    all_gather x1, waiting for transfers between devices, per_device(): lax.all_gather(attn_weight, 'wsh', axis=2, tiled=True)  197 us
    reduce_scatter x1, waiting for transfers between devices, per_device(): lax.psum_scatter(value_full, 'ctx', scatter_dimension=0, tiled=True)  133 us
    reduce_scatter x1, waiting for transfers between devices, per_device(): lax.psum_scatter(key_full, 'ctx', scatter_dimension=0, tiled=True)  126 us
    psum x1, waiting for transfers between devices, per_device(): model_grads, hidden_grads_out = lax.psum((shard_model, shard_hidden), 'ctx')  117 us
    all_gather x1, waiting for transfers between devices, per_device(): lax.all_gather(own_keys, 'ctx', axis=0, tiled=True)  67.9 us
    all_gather x1, waiting for transfers between devices, per_device(): lax.all_gather(own_values, 'ctx', axis=0, tiled=True)  67.7 us
    reduce_scatter x1, waiting for transfers between devices, per_device(): lax.psum_scatter(spread_model, 'wsh', scatter_dimension=2, tiled=True)  57 us
  transfers between devices with their start and end apart: 11, of which 10 were waited for; matrix products, arithmetic and copies ran while one was open for 8% of the time, Pallas kernels for 0%

commit v1 on v0

--- a/solution.py
+++ b/solution.py
@@ -185,7 +185,15 @@
         )
         return (gate_part, up_part)
 
-    weight_piece = lax.all_gather(mlp_weight, "wsh", axis=2, tiled=True)
+    ways, here = (lax.axis_size("wsh"), lax.axis_index("wsh"))
+    grown, reach = (mlp_weight, 1)
+    while reach < ways:
+        theirs = lax.ppermute(grown, "wsh", [(d, d ^ reach) for d in range(ways)])
+        mine_first = jnp.concatenate([grown, theirs], axis=2)
+        theirs_first = jnp.concatenate([theirs, grown], axis=2)
+        grown = jnp.where(here & reach == 0, mine_first, theirs_first)
+        reach = 2 * reach
+    weight_piece = grown
     adapt_piece = lax.all_gather(adapt_hidden, "wsh", axis=2, tiled=True)
     gathered_rows = pick_rows(adapt_piece, onehot, adapters)
     gate_part, up_part = gate_up_parts(weight_piece, gathered_rows)

time: 1720 us -> 2810 us (1.63)
  waiting for transfers between devices: 1390 us -> 2300 us
  other arithmetic: 33.2 us -> 181 us
  matrix products: 217 us -> 253 us
    ppermute x0 -> x2, waiting for transfers between devices: none -> 1570 us  [per_device(): theirs = lax.ppermute(grown, 'wsh', [(d, d ^ reach) for d in range(ways)])]
    all_gather x1, waiting for transfers between devices: 566 us -> 0.01 us  [per_device(): weight_piece = lax.all_gather(mlp_weight, 'wsh', axis=2, tiled=True)]
    select_n x0 -> x2, other arithmetic: none -> 146 us  [per_device(): grown = jnp.where(here & reach == 0, mine_first, theirs_first)]
    all_gather x1, waiting for transfers between devices: 67.9 us -> 0.02 us  [per_device(): lax.all_gather(own_keys, 'ctx', axis=0, tiled=True)]
  transfers between devices with their start and end apart: 11 -> 13, of which waited for: 10 -> 10; matrix products, arithmetic and copies ran while one was open for 8% -> 13% of each run, Pallas kernels for 0% -> 0%
where the time goes in v1:
time: 2810 us; the launch traced here: 2800 us
  waiting for transfers between devices  2300 us (82%)
  matrix products  253 us (9%)
  other arithmetic  181 us (6%)
  local copies, waits for them, and re-layouts  43.5 us (2%)
    ppermute x2, waiting for transfers between devices, per_device(): theirs = lax.ppermute(grown, 'wsh', [(d, d ^ reach) for d in range(ways)])  1570 us
    all_gather x1, waiting for transfers between devices, per_device(): lax.all_gather(attn_weight, 'wsh', axis=2, tiled=True)  197 us
    select_n x2, other arithmetic, per_device(): grown = jnp.where(here & reach == 0, mine_first, theirs_first)  146 us
    reduce_scatter x1, waiting for transfers between devices, per_device(): lax.psum_scatter(value_full, 'ctx', scatter_dimension=0, tiled=True)  133 us
    reduce_scatter x1, waiting for transfers between devices, per_device(): lax.psum_scatter(key_full, 'ctx', scatter_dimension=0, tiled=True)  123 us
    psum x1, waiting for transfers between devices, per_device(): model_grads, hidden_grads_out = lax.psum((shard_model, shard_hidden), 'ctx')  117 us
    reduce_scatter x1, waiting for transfers between devices, per_device(): lax.psum_scatter(spread_model, 'wsh', scatter_dimension=2, tiled=True)  56.9 us
  transfers between devices with their start and end apart: 13, of which 10 were waited for; matrix products, arithmetic and copies ran while one was open for 13% of the time, Pallas kernels for 0%

profile of v1, /device:TPU:0, one launch (start us, length us, event | category | flops | bytes accessed | tf_op | source)
XLA Modules:
  0.0 2804.1 jit_solution(10464396538050273572)
XLA Ops:
  7.9 11.5 copy.32
  20.4 6.4 all_gather.25
  30.2 9.2 all-gather.10.cloned.1.call-done
  39.4 4.7 fusion.23
  45.8 196.8 %all-gather.8.cloned.1.call-done = bf16[4,2048,2048]{1,2,0:T(8,128)(2,1)} async-done(((bf16[4,2048,512]{1,2,0:T(8,128)(2,1)}), bf16[4,2048,2048]{1,2,0:T(8,128)(2,1)}) %all-gather.8.cloned.1.call-update) | async-done | bytes 33554448 | tf_op jit(solution)/shard_map/all_gather | solution.py:115
  242.6 11.9 fusion.79
  257.7 2.7 copy.34
  260.4 2.5 copy.35
  272.7 37.2 %collective-permute-done = bf16[3,2048,2048]{2,1,0:T(8,128)(2,1)} collective-permute-done((bf16[3,2048,2048]{2,1,0:T(8,128)(2,1)}, bf16[3,2048,2048]{2,1,0:T(8,128)(2,1)}, u32[]{:S(2)}, u32[]{:S(2)}) %collective-permute-start) | collective-permute-done | bytes 25165856 | tf_op jit(solution)/shard_map/ppermute | solution.py:191
  309.9 49.8 %maximum_select_fusion.1 = bf16[3,2048,4096]{2,1,0:T(8,128)(2,1)} fusion(bf16[3,2048,2048]{2,1,0:T(8,128)(2,1)} %collective-permute-done, bf16[3,2048,2048]{2,1,0:T(8,128)(2,1)} %param.13, pred[]{:T(512)S(6)} %eq.19), kind=kLoop, calls=%fused_computation.1 | loop fusion | flops 226492416 | bytes 100663296 | tf_op jit(solution)/shard_map/jit(_where)/select_n | solution.py:194
  361.0 6.6 fusion.21
  368.5 4.3 fusion.18
  376.2 48.9 %all-gather.18.cloned.1.call-done = bf16[1,1024,2048]{1,2,0:T(8,128)(2,1)} async-done(((bf16[1,128,2048]{1,2,0:T(8,128)(2,1)}), bf16[1,1024,2048]{1,2,0:T(8,128)(2,1)}) %all-gather.18.cloned.1.call-update) | async-done | bytes 4194320 | tf_op jit(solution)/shard_map/all_gather | solution.py:141
  425.1 7.2 convolution_convert_fusion
  432.6 9.4 fusion.17
  444.0 3.9 convolution_multiply_fusion.1
  447.9 3.9 convolution_multiply_fusion
  451.8 1529.1 %collective-permute-done.1 = bf16[3,2048,4096]{2,1,0:T(8,128)(2,1)} collective-permute-done((bf16[3,2048,4096]{2,1,0:T(8,128)(2,1)}, bf16[3,2048,4096]{2,1,0:T(8,128)(2,1)}, u32[]{:S(2)}, u32[]{:S(2)}) %collective-permute-start.1) | collective-permute-done | bytes 50331680 | tf_op jit(solution)/shard_map/ppermute | solution.py:191
  1980.9 96.1 %maximum_select_fusion = bf16[3,2048,8192]{2,1,0:T(8,128)(2,1)} fusion(bf16[3,2048,4096]{2,1,0:T(8,128)(2,1)} %collective-permute-done.1, bf16[3,2048,4096]{2,1,0:T(8,128)(2,1)} %maximum_select_fusion.1, pred[]{:T(512)S(6)} %eq.18), kind=kLoop, calls=%fused_computation | loop fusion | flops 452984832 | bytes 201326592 | tf_op jit(solution)/shard_map/jit(_where)/select_n | solution.py:194
  2077.0 16.2 fusion.12
  2093.2 15.1 multiply_convert_fusion.4
  2110.7 19.3 fusion.59
  2131.9 15.0 fusion
  2146.9 4.9 convolution_add_fusion
  2151.8 16.2 fusion.11
  2168.0 18.7 multiply_convert_fusion.3
  2188.0 17.0 fusion.4
  2205.0 16.3 fusion.41
  2225.3 4.7 fusion.16
  2231.5 8.2 multiply_reduce_fusion
  2239.8 2.5 multiply_convert_fusion
  2242.3 4.7 broadcast_multiply_fusion
  2247.1 9.4 fusion.86
  2260.1 3.5 convolution_bitcast_fusion
  2263.6 3.4 bitcast_multiply_fusion
  2267.1 4.8 fusion.49
  2271.9 123.2 %reduce-scatter.5.cloned.1.call-done = f32[128,2048]{0,1:T(8,128)} async-done(((f32[1024,2048]{0,1:T(8,128)}), f32[128,2048]{0,1:T(8,128)}) %reduce-scatter.5.cloned.1.call-update) | async-done | bytes 1048592 | tf_op jit(solution)/shard_map/reduce_scatter | solution.py:319
  2402.2 2.7 copy.41
  2404.8 3.0 pad_maximum_fusion.3
  2407.8 2.5 copy.46
  2412.3 133.3 %reduce-scatter.7.cloned.1.call-done = f32[128,2048]{0,1:T(8,128)} async-done(((f32[1024,2048]{0,1:T(8,128)}), f32[128,2048]{0,1:T(8,128)}) %reduce-scatter.7.cloned.1.call-update) | async-done | bytes 1048592 | tf_op jit(solution)/shard_map/reduce_scatter | solution.py:320
  2552.5 3.3 bitcast_multiply_fusion.1
  2555.8 49.4 %reduce-scatter.11.cloned.1.call-done = f32[3,64,2048]{2,1,0:T(8,128)} async-done(((f32[3,64,8192]{2,1,0:T(8,128)}), f32[3,64,2048]{2,1,0:T(8,128)}) %reduce-scatter.11.cloned.1.call-update) | async-done | bytes 1572880 | tf_op jit(solution)/shard_map/reduce_scatter | solution.py:367
  2605.2 56.9 %reduce-scatter.9.cloned.1.call-done = f32[11,64,512]{2,1,0:T(8,128)} async-done(((f32[11,64,2048]{2,1,0:T(8,128)}), f32[11,64,512]{2,1,0:T(8,128)}) %reduce-scatter.9.cloned.1.call-update) | async-done | bytes 1441808 | tf_op jit(solution)/shard_map/reduce_scatter | solution.py:366
  2663.5 11.3 fusion.35
  2674.8 117.3 %all-reduce.3.cloned.1.call-done = (f32[11,64,512]{2,1,0:T(8,128)}, f32[3,64,2048]{2,1,0:T(8,128)}) async-done(((f32[11,64,512]{2,1,0:T(8,128)}, f32[3,64,2048]{2,1,0:T(8,128)}), (f32[11,64,512]{2,1,0:T(8,128)}, f32[3,64,2048]{2,1,0:T(8,128)})) %all-reduce.3.cloned.1.call-update) | async-done | bytes 3014672 | tf_op jit(solution)/shard_map/psum | solution.py:369
  2792.1 2.6 copy.86
  2794.7 2.7 copy.87
  (250 shorter events, 58.9 us)
Async XLA Ops:
  7.2 32.2 %all-gather.10.cloned.1.call-start = ((), (), s32[]{:S(2)}) async-start(), calls=%async_computation.5 | async-start | bytes 3604480 | tf_op jit(solution)/shard_map/all_gather | solution.py:117
  7.9 234.7 %all-gather.8.cloned.1.call-start = ((), (), s32[]{:S(2)}) async-start(), calls=%async_computation.4 | async-start | bytes 41943040 | tf_op jit(solution)/shard_map/all_gather | solution.py:115
  19.5 9.9 copy-start.72
  19.5 341.5 %all-gather.14.cloned.1.call-start = ((), (), s32[]{:S(2)}) async-start(), calls=%async_computation.7 | async-start | bytes 3932160 | tf_op jit(solution)/shard_map/all_gather | solution.py:197
  20.2 348.3 %all-gather.12.cloned.1.call-start = ((), (), s32[]{:S(2)}) async-start(), calls=%async_computation.6 | async-start | bytes 4718592 | tf_op jit(solution)/shard_map/all_gather | solution.py:140
  27.5 236.4 %copy-start.44 = (f32[1,2048]{1,0:T(1,128)}, f32[1,2048]{1,0:T(1,128)S(1)}, u32[]{:S(2)}) copy-start(f32[1,2048]{1,0:T(1,128)S(1)} %get-tuple-element.38) | copy-start | bytes 24580
  27.5 237.8 %copy-start.46 = (f32[1,2048]{1,0:T(1,128)}, f32[1,2048]{1,0:T(1,128)S(1)}, u32[]{:S(2)}) copy-start(f32[1,2048]{1,0:T(1,128)S(1)} %get-tuple-element.39) | copy-start | bytes 24580
  27.5 415.5 %copy-start.48 = (f32[1,2048]{1,0:T(1,128)}, f32[1,2048]{1,0:T(1,128)S(1)}, u32[]{:S(2)}) copy-start(f32[1,2048]{1,0:T(1,128)S(1)} %get-tuple-element.37) | copy-start | bytes 24580
  30.2 235.3 %copy-start.32 = (f32[128,64]{1,0:T(8,128)}, f32[128,64]{1,0:T(8,128)S(1)}, u32[]{:S(2)}) copy-start(f32[128,64]{1,0:T(8,128)S(1)} %get-tuple-element.40) | copy-start | bytes 98308
  30.2 235.3 %copy-start.34 = (f32[128,64]{1,0:T(8,128)}, f32[128,64]{1,0:T(8,128)S(1)}, u32[]{:S(2)}) copy-start(f32[128,64]{1,0:T(8,128)S(1)} %get-tuple-element.41) | copy-start | bytes 98308
  45.8 208.7 %copy-start.53 = (bf16[3,16,128]{2,1,0:T(8,128)(2,1)}, bf16[3,16,128]{2,1,0:T(8,128)(2,1)S(1)}, u32[]{:S(2)}) copy-start(bf16[3,16,128]{2,1,0:T(8,128)(2,1)S(1)} %convolution_convert_fusion.1) | copy-start | bytes 36868
  256.1 14.3 copy-start.1
  270.4 154.8 %all-gather.18.cloned.1.call-start = ((), (), s32[]{:S(2)}) async-start(), calls=%async_computation.13 | async-start | bytes 4718592 | tf_op jit(solution)/shard_map/all_gather | solution.py:141
  271.3 1860.7 %all-gather.16.cloned.1.call-start = ((), (), s32[]{:S(2)}) async-start(), calls=%async_computation.8 | async-start | bytes 125829120 | tf_op jit(solution)/shard_map/all_gather | solution.py:227
  271.9 2123.2 %reduce-scatter.5.cloned.1.call-start = ((), (), s32[]{:S(2)}) async-start(), calls=%async_computation.9 | async-start | bytes 9437184 | tf_op jit(solution)/shard_map/reduce_scatter | solution.py:319
  272.4 37.6 %collective-permute-start = (bf16[3,2048,2048]{2,1,0:T(8,128)(2,1)}, bf16[3,2048,2048]{2,1,0:T(8,128)(2,1)}, u32[]{:S(2)}, u32[]{:S(2)}) collective-permute-start(bf16[3,2048,2048]{2,1,0:T(8,128)(2,1)} %param.13), channel_id=1, source_target_pairs={{0,1},{1,0},{2,3},{3,2},{4,5},{5,4},{6,7},{7,6},{8,9},{9,8},{10,11... | collective-permute-start | bytes 75497480 | tf_op jit(solution)/shard_map/ppermute | solution.py:191
  359.8 1621.1 %collective-permute-start.1 = (bf16[3,2048,4096]{2,1,0:T(8,128)(2,1)}, bf16[3,2048,4096]{2,1,0:T(8,128)(2,1)}, u32[]{:S(2)}, u32[]{:S(2)}) collective-permute-start(bf16[3,2048,4096]{2,1,0:T(8,128)(2,1)} %maximum_select_fusion.1), channel_id=1, source_target_pairs={{0,2},{1,3},{2,0},{3,1},{4,6},{5,7},{6,4},{7,5},{8,10},{9,11},{10,... | collective-permute-start | bytes 150994944 | tf_op jit(solution)/shard_map/ppermute | solution.py:191
  360.9 64.2 %copy-start.13 = (pred[128,1024]{1,0:T(8,128)(4,1)}, pred[128,1024]{1,0:T(8,128)(4,1)S(1)}, u32[]{:S(2)}) copy-start(pred[128,1024]{1,0:T(8,128)(4,1)S(1)} %compare_and_fusion) | copy-start | bytes 393220
  376.2 56.1 %copy-start.42 = (f32[16,128]{1,0:T(8,128)}, f32[16,128]{1,0:T(8,128)S(1)}, u32[]{:S(2)}) copy-start(f32[16,128]{1,0:T(8,128)S(1)} %log_add_fusion) | copy-start | bytes 24580
  432.3 9.6 copy-start.29
  432.5 9.4 copy-start.55
  432.5 10.9 copy-start.7
  442.3 9.4 copy-start.4
  443.7 1724.3 %copy-start.15 = (bf16[128,2048]{1,0:T(8,128)(2,1)}, bf16[128,2048]{1,0:T(8,128)(2,1)S(1)}, u32[]{:S(2)}) copy-start(bf16[128,2048]{1,0:T(8,128)(2,1)S(1)} %fusion.73) | copy-start | bytes 1572868
  2093.2 17.5 copy-start.52
  2093.2 17.5 copy-start.66
  2110.3 19.6 copy-start.57
  2131.7 15.2 copy-start.17
  2205.0 16.4 copy-start.5
  2205.0 16.4 copy-start.49
  2205.0 17.7 copy-start.8
  2205.0 17.7 copy-start.26
  2205.0 17.8 copy-start.65
  2205.0 17.8 copy-start.69
  2247.0 298.6 %reduce-scatter.7.cloned.1.call-start = ((), (), s32[]{:S(2)}) async-start(), calls=%async_computation.10 | async-start | bytes 9437184 | tf_op jit(solution)/shard_map/reduce_scatter | solution.py:320
  2256.5 348.7 %reduce-scatter.11.cloned.1.call-start = ((), (), s32[]{:S(2)}) async-start(), calls=%async_computation.12 | async-start | bytes 7864320 | tf_op jit(solution)/shard_map/reduce_scatter | solution.py:367
  2267.0 395.2 %reduce-scatter.9.cloned.1.call-start = ((), (), s32[]{:S(2)}) async-start(), calls=%async_computation.11 | async-start | bytes 7208960 | tf_op jit(solution)/shard_map/reduce_scatter | solution.py:366
  2271.8 127.0 %copy-start.33 = (f32[128,64]{1,0:T(8,128)S(1)}, f32[128,64]{1,0:T(8,128)}, u32[]{:S(2)}) copy-start(f32[128,64]{1,0:T(8,128)} %copy-done.32) | copy-start | bytes 98308
  2271.8 127.0 %copy-start.35 = (f32[128,64]{1,0:T(8,128)S(1)}, f32[128,64]{1,0:T(8,128)}, u32[]{:S(2)}) copy-start(f32[128,64]{1,0:T(8,128)} %copy-done.34) | copy-start | bytes 98308
  2407.8 139.1 %copy-start.60 = (f32[128]{0:T(128)S(1)}, f32[128]{0:T(128)}, u32[]{:S(2)}) copy-start(f32[128]{0:T(128)} %copy-done.59) | copy-start | bytes 1540
  2407.8 139.1 %copy-start.62 = (f32[128]{0:T(128)S(1)}, f32[128]{0:T(128)}, u32[]{:S(2)}) copy-start(f32[128]{0:T(128)} %copy-done.61) | copy-start | bytes 1540
  2407.8 139.1 %copy-start.67 = (f32[128]{0:T(128)S(1)}, f32[128]{0:T(128)}, u32[]{:S(2)}) copy-start(f32[128]{0:T(128)} %get-tuple-element.44) | copy-start | bytes 1540
  2407.8 139.1 %copy-start.68 = (f32[128]{0:T(128)S(1)}, f32[128]{0:T(128)}, u32[]{:S(2)}) copy-start(f32[128]{0:T(128)} %get-tuple-element.61) | copy-start | bytes 1540
  2555.8 107.7 %copy-start.28 = (f32[128,2048]{1,0:T(8,128)S(1)}, f32[128,2048]{1,0:T(8,128)}, u32[]{:S(2)}) copy-start(f32[128,2048]{1,0:T(8,128)} %copy-done.27) | copy-start | bytes 3145732
  2555.8 107.7 %copy-start.37 = (bf16[1,128,2048]{1,2,0:T(8,128)(2,1)S(1)}, bf16[1,128,2048]{1,2,0:T(8,128)(2,1)}, u32[]{:S(2)}) copy-start(bf16[1,128,2048]{1,2,0:T(8,128)(2,1)} %copy-done.36) | copy-start | bytes 1572868
  2555.8 107.7 %copy-start.39 = (bf16[1,128,2048]{1,2,0:T(8,128)(2,1)S(1)}, bf16[1,128,2048]{1,2,0:T(8,128)(2,1)}, u32[]{:S(2)}) copy-start(bf16[1,128,2048]{1,2,0:T(8,128)(2,1)} %copy-done.38) | copy-start | bytes 1572868
  2555.8 107.7 %copy-start.41 = (bf16[1,128,2048]{1,2,0:T(8,128)(2,1)S(1)}, bf16[1,128,2048]{1,2,0:T(8,128)(2,1)}, u32[]{:S(2)}) copy-start(bf16[1,128,2048]{1,2,0:T(8,128)(2,1)} %copy-done.40) | copy-start | bytes 1572868
  2555.8 236.4 %all-reduce.3.cloned.1.call-start = ((), (), s32[]{:S(2)}) async-start(), calls=%async_computation.14 | async-start | bytes 6029312 | tf_op jit(solution)/shard_map/psum | solution.py:369
  (41 other events, 170.6 us)
Sparse Core Ops, SparseCore 0:
  9.5 29.8 all-gather.9
  41.0 201.5 all-gather.7
  244.1 28.4 all-gather.13
  275.2 74.6 all-gather.11
  352.3 72.7 all-gather.17
  426.6 1121.4 all-gather.15
  2247.2 147.8 reduce-scatter.4
  2398.6 146.9 reduce-scatter.6
  2548.2 57.0 reduce-scatter.10
  2607.6 54.5 reduce-scatter.8
  2666.0 126.1 all-reduce.2
